TPU v7x, 32 devices: a whole 2x2x4 slice. The times are simulated.
32 devices in a mesh: region: 4 (over z), row: 2 (over core), col: 4 (over y, x).
Axes of the slice: x: 2, y: 2, z: 4, core: 2. Of those that a mesh axis runs over, the one named last changes fastest.
Arguments:
- cam_jac: bfloat16 [3, 2, 256, 16384], P(None, None, None, 'region'), may hold values from -1 to 1
- point_rows: bfloat16 [3, 2, 4, 16384], P(None, None, None, 'region'), may hold values from -6 to 6
- track_images: int32 [3, 16384], P(None, 'region'), may hold values from 0 to 3, as said below
- track_counts: int32 [4], replicated, may hold values from 1 to 4096, 8192 in all
Outputs:
- factor: float32 [1024, 1024], P(('region', 'row'), 'col')
- solved: float32 [1024], replicated
Inputs may be any that keep to these rules, and one draw needn't show every extreme that they name: `track_images`: each track's 3 entries are different images of the slab. `track_counts`: entry r counts region r's live tracks, which fill its first slots; later slots hold data that no output reads. The counts sum to 8192, and one region has exactly 4096.
All inputs are finite; a program needn't handle non-finite values.
Results may differ from a plain program's by a relative error of at most 0.0036.
Values may be sent and summed in bfloat16 or wider, within the bound.
A program may use at most 128 MiB of HBM per device.

v0:
```python
import jax
import jax.numpy as jnp
from jax import lax
from jax.sharding import PartitionSpec as P

SLAB_IMAGES = 4
BLOCK = 256


damping = 0.1
point_damping = 0.5


def from_root(value, axis, source):
    kept = jnp.where(lax.axis_index(axis) == source, value, 0).astype(value.dtype)
    return lax.psum(kept, axis)


def lower_solve(factor_parts, first, second, third):
    diag_one, below_one, diag_two, below_far, below_two, diag_three = factor_parts
    out_one = first / diag_one
    out_two = (second - below_one * out_one) / diag_two
    out_three = (third - below_far * out_one - below_two * out_two) / diag_three
    return (out_one, out_two, out_three)


def block_terms(cam, points, selector):
    jac_point = points[:, :, 0:3].astype(jnp.float32)
    errors = points[:, :, 3].astype(jnp.float32)

    def entry(left, right):
        return jnp.sum(jac_point[:, :, left] * jac_point[:, :, right], axis=(0, 1))

    diag_one = jnp.sqrt(entry(0, 0) + point_damping)
    below_one = entry(1, 0) / diag_one
    below_far = entry(2, 0) / diag_one
    diag_two = jnp.sqrt(entry(1, 1) + point_damping - below_one * below_one)
    below_two = (entry(2, 1) - below_far * below_one) / diag_two
    diag_three = jnp.sqrt(
        entry(2, 2) + point_damping - below_far * below_far - below_two * below_two
    )
    factor_parts = (diag_one, below_one, diag_two, below_far, below_two, diag_three)
    coef = jnp.stack(
        lower_solve(factor_parts, jac_point[:, :, 0], jac_point[:, :, 1], jac_point[:, :, 2]),
        axis=0,
    ).astype(jnp.bfloat16)
    grads = [jnp.sum(jac_point[:, :, comp] * errors, axis=(0, 1)) for comp in range(3)]
    point_step = jnp.stack(lower_solve(factor_parts, grads[0], grads[1], grads[2]), axis=0).astype(
        jnp.bfloat16
    )
    coef_wide = coef.astype(jnp.float32)
    products = (
        cam[:, 0, :, None, :].astype(jnp.float32)
        * coef_wide[:, :, 0, :].transpose(1, 0, 2)[:, None, :, :]
    )
    products = (
        products
        + cam[:, 1, :, None, :].astype(jnp.float32)
        * coef_wide[:, :, 1, :].transpose(1, 0, 2)[:, None, :, :]
    )
    schur = selector[0][:, None, None, :] * products[0][None]
    for view in range(1, selector.shape[0]):
        schur = schur + selector[view][:, None, None, :] * products[view][None]
    schur = schur.astype(jnp.bfloat16)
    pick = selector.astype(jnp.bfloat16)
    diagonal = jnp.einsum("krpb,kab->aprb", cam, pick, preferred_element_type=jnp.float32).astype(
        jnp.bfloat16
    )
    err_pick = (errors[None, :, :, :] * selector.transpose(1, 0, 2)[:, :, None, :]).astype(
        jnp.bfloat16
    )
    direct = jnp.einsum("krpb,akrb->ap", cam, err_pick, preferred_element_type=jnp.float32)
    coupled = jnp.einsum("apmb,mb->ap", schur, point_step, preferred_element_type=jnp.float32)
    return (schur, diagonal, direct - coupled)


def panel_factor(column, first_row, end_row):
    chol_block = jnp.linalg.cholesky(column[first_row:end_row])
    parts = [jnp.zeros((first_row, column.shape[1]), column.dtype), chol_block]
    if end_row < column.shape[0]:
        parts.append(
            lax.linalg.triangular_solve(
                chol_block, column[end_row:], left_side=False, lower=True, transpose_a=True
            )
        )
    return jnp.concatenate(parts, axis=0)


def on_device(cam_jac, point_rows, track_images, track_counts):
    regions = lax.axis_size("region")
    row_count = lax.axis_size("row")
    region_at = lax.axis_index("region")
    row_at = lax.axis_index("row")
    col_at = lax.axis_index("col")
    params = cam_jac.shape[2]
    slots = cam_jac.shape[3]
    total_cols = SLAB_IMAGES * params
    row_block = total_cols // (regions * row_count)
    images = track_images.astype(jnp.float32)
    live = (jnp.arange(slots, dtype=jnp.int32) < track_counts[region_at]).astype(jnp.float32)
    depth = live.shape[0]
    tile_rows = regions * row_block
    share = params // row_count
    contract = (((1,), (1,)), ((), ()))

    def block_step(block, carry):
        tile_acc, grad_acc = carry
        start = block * BLOCK
        cam = lax.dynamic_slice_in_dim(cam_jac, start, BLOCK, 3)
        pts = lax.dynamic_slice_in_dim(point_rows, start, BLOCK, 3)
        block_images = lax.dynamic_slice_in_dim(images, start, BLOCK, 1)
        alive = lax.dynamic_slice_in_dim(live, start, BLOCK, 0)
        selector = (
            block_images[:, None, :] == jnp.arange(SLAB_IMAGES, dtype=jnp.float32)[None, :, None]
        ).astype(jnp.float32) * alive[None, None, :]
        schur, diagonal, grad = block_terms(cam, pts, selector)
        schur_grid = schur.reshape(regions, row_count, row_block, 3 * BLOCK)
        row_part = lax.dynamic_index_in_dim(schur_grid, row_at, 1, keepdims=False).reshape(
            tile_rows, 3 * BLOCK
        )
        col_part = lax.dynamic_index_in_dim(schur, col_at, 0, keepdims=False).reshape(
            params, 3 * BLOCK
        )
        tile_acc = tile_acc - lax.dot_general(
            row_part, col_part, contract, preferred_element_type=jnp.float32
        )
        diag_grid = diagonal.reshape(regions, row_count, row_block, 2 * BLOCK)
        diag_rows = lax.dynamic_index_in_dim(diag_grid, row_at, 1, keepdims=False).reshape(
            tile_rows, 2 * BLOCK
        )
        diag_rows = lax.dynamic_slice_in_dim(diag_rows, col_at * share, share, 0)
        diag_col = lax.dynamic_index_in_dim(diagonal, col_at, 0, keepdims=False).reshape(
            params, 2 * BLOCK
        )
        update = lax.dot_general(diag_rows, diag_col, contract, preferred_element_type=jnp.float32)
        current = lax.dynamic_slice_in_dim(tile_acc, col_at * share, share, 0)
        tile_acc = lax.dynamic_update_slice_in_dim(tile_acc, current + update, col_at * share, 0)
        grad_acc = grad_acc + lax.dynamic_index_in_dim(grad, col_at, 0, keepdims=False)
        return (tile_acc, grad_acc)

    start_state = (jnp.zeros((tile_rows, params), jnp.float32), jnp.zeros((params,), jnp.float32))
    tile_acc, grad_acc = lax.fori_loop(0, depth // BLOCK, block_step, start_state)
    held, grad_piece = (
        lax.psum_scatter(tile_acc, "region", scatter_dimension=0, tiled=True),
        lax.psum_scatter(
            grad_acc.reshape(regions, params // regions), "region", scatter_dimension=0, tiled=True
        ),
    )
    gathered = lax.all_gather(grad_piece, ("region", "col"), axis=0, tiled=True)
    gradient = (
        gathered.reshape(regions, SLAB_IMAGES, params // regions)
        .transpose(1, 0, 2)
        .reshape(total_cols)
    )
    row_start = (region_at * row_count + row_at) * row_block
    global_rows = row_start + jnp.arange(row_block, dtype=jnp.int32)
    global_cols = col_at * params + jnp.arange(params, dtype=jnp.int32)
    held = held + damping * (global_rows[:, None] == global_cols[None, :]).astype(jnp.float32)
    factor_mine = jnp.zeros((row_block, params), jnp.float32)
    pieces = []
    for panel in range(SLAB_IMAGES):
        first_row = panel * params
        end_row = first_row + params
        column = lax.all_gather(held, ("region", "row"), axis=0, tiled=True)
        factored = lax.cond(
            col_at == panel,
            lambda whole: panel_factor(whole, first_row, end_row),
            lambda whole: jnp.zeros_like(whole),
            column,
        )
        factored = from_root(factored, "col", panel)
        mine = lax.dynamic_slice_in_dim(factored, row_start, row_block, 0)
        partner = lax.dynamic_slice_in_dim(factored, col_at * params, params, 0)
        held = held - jnp.dot(mine, partner.T, precision=lax.Precision.HIGHEST)
        factor_mine = jnp.where(col_at == panel, mine, factor_mine)
        part_z = lax.linalg.triangular_solve(
            factored[first_row:end_row],
            gradient[first_row:end_row][:, None],
            left_side=True,
            lower=True,
        )[:, 0]
        pieces.append(part_z)
        below = jnp.concatenate(
            [jnp.zeros((end_row, params), jnp.float32), factored[end_row:]], axis=0
        )
        gradient = gradient - jnp.dot(below, part_z, precision=lax.Precision.HIGHEST)
    return (factor_mine, jnp.concatenate(pieces))


def solution(mesh):
    in_specs = (
        P(None, None, None, "region"),
        P(None, None, None, "region"),
        P(None, "region"),
        P(),
    )
    out_specs = (P(("region", "row"), "col"), P())
    return jax.shard_map(
        on_device, mesh=mesh, in_specs=in_specs, out_specs=out_specs, check_vma=False
    )
```

profile of v0, /device:TPU:15, one launch (start us, length us, event | category | flops | bytes accessed | tf_op | source)
XLA Modules:
  0.0 1094.6 jit_solution(16919428303074503304)
XLA Ops:
  11.4 459.8 %while.32 = (s32[]{:T(128)}, f32[512,256]{1,0:T(8,128)}, f32[256]{0:T(256)}, f32[3,4096]{1,0:T(4,128)S(1)}, f32[4096]{0:T(1024)}, /*index=5*/bf16[3,2,256,4096]{...) while((s32[]{:T(128)}, f32[512,256]{1,0:T(8,128)}, ...), condition=%wide.region_10.11_spmd.clone, body=%wide.region_0.10_spmd.clone.sunk | while | flops 252784384 | bytes 64036492 | solution.py:142
  107.4 1.9 copy.167
  251.1 1.9 copy.167
  308.5 1.9 copy.167
  337.3 1.9 copy.167
  471.3 18.8 %reduce-scatter.2.cloned.1.call-done = f32[128,256]{1,0:T(8,128)} async-done(((f32[512,256]{1,0:T(8,128)}), f32[128,256]{1,0:T(8,128)}) %reduce-scatter.2.cloned.1.call-update) | async-done | bytes 131088 | tf_op jit(solution)/shard_map/reduce_scatter | solution.py:144
  491.8 25.6 %all-gather.6.cloned.1.call-done = f32[1024,256]{1,0:T(8,128)} async-done(((f32[128,256]{1,0:T(8,128)}), f32[1024,256]{1,0:T(8,128)}) %all-gather.6.cloned.1.call-update) | async-done | bytes 1048592 | tf_op jit(solution)/shard_map/all_gather | solution.py:164
  517.5 8.0 conditional.4
  526.6 105.4 %all-reduce.11.cloned.1.call-done = f32[1024,256]{1,0:T(8,128)} async-done(((f32[1024,256]{1,0:T(8,128)}), f32[1024,256]{1,0:T(8,128)}) %all-reduce.11.cloned.1.call-update) | async-done | bytes 1048592 | tf_op jit(solution)/shard_map/psum | solution.py:16
  632.1 2.1 convolution_subtract_fusion.10
  634.3 23.9 %all-gather.8.cloned.1.call-done = f32[1024,256]{1,0:T(8,128)} async-done(((f32[128,256]{1,0:T(8,128)}), f32[1024,256]{1,0:T(8,128)}) %all-gather.8.cloned.1.call-update) | async-done | bytes 1048592 | tf_op jit(solution)/shard_map/all_gather | solution.py:164
  658.2 8.4 conditional.5
  667.7 106.0 %all-reduce.13.cloned.1.call-done = f32[1024,256]{1,0:T(8,128)} async-done(((f32[1024,256]{1,0:T(8,128)}), f32[1024,256]{1,0:T(8,128)}) %all-reduce.13.cloned.1.call-update) | async-done | bytes 1048592 | tf_op jit(solution)/shard_map/psum | solution.py:16
  773.7 2.1 convolution_subtract_fusion.9
  776.6 6.9 all-reduce.5
  784.1 23.0 %all-gather = f32[16,1,64]{2,1,0:T(1,128)S(1)} all-gather(f32[1,1,64]{2,1,0:T(1,128)S(1)} %dynamic-slice_bitcast_fusion.1), channel_id=1, replica_groups=mesh['region'=4,'row'=2,'col'=4] {'region','col'}, dimensions={0}, use_global_device_ids=true | all-gather | bytes 4352 | tf_op jit(solution)/shard_map/all_gather | solution.py:149
  807.3 5.4 conditional.6
  813.9 3.9 while.33
  817.8 19.7 %custom-call.31 = f32[2,128,128]{1,2,0:T(8,128)S(1)} custom-call(f32[2,128,128]{2,1,0:T(8,128)S(1)} %get-tuple-element.332), custom_call_target="InvertDiagBlocksLowerTriangular" | custom-call | tf_op jit(solution)/shard_map/triangular_solve/custom-call.6 | solution.py:176
  838.8 101.0 %all-reduce.15.cloned.1.call-done = f32[1024,256]{1,0:T(8,128)} async-done(((f32[1024,256]{1,0:T(8,128)}), f32[1024,256]{1,0:T(8,128)}) %all-reduce.15.cloned.1.call-update) | async-done | bytes 1048592 | tf_op jit(solution)/shard_map/psum | solution.py:16
  939.9 2.1 convolution_subtract_fusion.8
  942.1 3.8 while.34
  945.9 19.7 %custom-call.32 = f32[2,128,128]{1,2,0:T(8,128)S(1)} custom-call(f32[2,128,128]{2,1,0:T(8,128)S(1)} %get-tuple-element.333), custom_call_target="InvertDiagBlocksLowerTriangular" | custom-call | tf_op jit(solution)/shard_map/triangular_solve/custom-call.6 | solution.py:176
  967.9 38.6 %conditional.7 = (f32[1024,256]{1,0:T(8,128)S(1)}) conditional(s32[]{:T(128)} %convert_element_type.159, () %tuple.55, f32[1024,256]{1,0:T(8,128)} %all-gather.12.cloned.1.call-done), branch_computations={%region_25.27_spmd, %region_26.28_spmd} | conditional | flops 50807040 | bytes 4917270 | solution.py:165
  970.5 11.7 %cholesky.316 = f32[128,128]{1,0:T(8,128)S(1)} custom-call(f32[128,128]{1,0:T(8,128)S(1)} %cholesky.355), custom_call_target="Cholesky" | custom-call | tf_op jit(solution)/shard_map/cond/branch_1_fun/jit(cholesky)/cholesky | solution.py:78
  982.2 9.8 custom-call.30
  992.5 11.7 %cholesky.333 = f32[128,128]{1,0:T(8,128)S(1)} custom-call(f32[128,128]{1,0:T(8,128)S(1)} %convolution_subtract_fusion.6), custom_call_target="Cholesky" | custom-call | tf_op jit(solution)/shard_map/cond/branch_1_fun/jit(cholesky)/cholesky | solution.py:78
  1007.6 4.0 while.35
  1011.6 19.7 %custom-call.33 = f32[2,128,128]{1,2,0:T(8,128)S(1)} custom-call(f32[2,128,128]{2,1,0:T(8,128)S(1)} %get-tuple-element.334), custom_call_target="InvertDiagBlocksLowerTriangular" | custom-call | tf_op jit(solution)/shard_map/triangular_solve/custom-call.6 | solution.py:176
  1032.3 28.0 %all-reduce.17.cloned.1.call-done = f32[1024,256]{1,0:T(8,128)} async-done(((f32[1024,256]{1,0:T(8,128)}), f32[1024,256]{1,0:T(8,128)}) %all-reduce.17.cloned.1.call-update) | async-done | bytes 1048592 | tf_op jit(solution)/shard_map/psum | solution.py:16
  1061.3 4.0 while.36
  1065.3 19.7 %custom-call.34 = f32[2,128,128]{1,2,0:T(8,128)S(1)} custom-call(f32[2,128,128]{2,1,0:T(8,128)S(1)} %get-tuple-element.335), custom_call_target="InvertDiagBlocksLowerTriangular" | custom-call | tf_op jit(solution)/shard_map/triangular_solve/custom-call.6 | solution.py:176
  (1488 shorter events, 485.6 us)
Async XLA Ops:
  7.2 482.9 %reduce-scatter.2.cloned.1.call-start = ((), (), s32[]{:S(2)}) async-start(), calls=%async_computation.1 | async-start | bytes 655360 | tf_op jit(solution)/shard_map/reduce_scatter | solution.py:144
  11.4 5.8 copy-start.17
  40.1 5.8 copy-start.17
  68.9 5.8 copy-start.17
  97.7 5.8 copy-start.17
  126.4 5.8 copy-start.17
  155.1 5.8 copy-start.17
  183.9 5.8 copy-start.17
  212.6 5.8 copy-start.17
  241.3 5.8 copy-start.17
  270.1 5.8 copy-start.17
  327.5 5.8 copy-start.17
  356.2 5.8 copy-start.17
  385.0 5.8 copy-start.17
  413.7 5.8 copy-start.17
  442.4 5.8 copy-start.17
  471.2 46.3 %all-gather.6.cloned.1.call-start = ((), (), s32[]{:S(2)}) async-start(), calls=%async_computation.2 | async-start | bytes 1179648 | tf_op jit(solution)/shard_map/all_gather | solution.py:164
  491.8 140.3 %all-reduce.11.cloned.1.call-start = ((), (), s32[]{:S(2)}) async-start(), calls=%async_computation.3 | async-start | bytes 2097152 | tf_op jit(solution)/shard_map/psum | solution.py:16
  525.5 106.6 %copy-start.10 = (f32[128,256]{1,0:T(8,128)S(1)}, f32[128,256]{1,0:T(8,128)}, u32[]{:S(2)}) copy-start(f32[128,256]{1,0:T(8,128)} %select_add_fusion.1) | copy-start | bytes 393220
  526.6 131.6 %all-gather.8.cloned.1.call-start = ((), (), s32[]{:S(2)}) async-start(), calls=%async_computation.4 | async-start | bytes 1179648 | tf_op jit(solution)/shard_map/all_gather | solution.py:164
  634.2 139.5 %all-reduce.13.cloned.1.call-start = ((), (), s32[]{:S(2)}) async-start(), calls=%async_computation.5 | async-start | bytes 2097152 | tf_op jit(solution)/shard_map/psum | solution.py:16
  666.6 107.2 %copy-start.9 = (f32[128,256]{1,0:T(8,128)S(1)}, f32[128,256]{1,0:T(8,128)}, u32[]{:S(2)}) copy-start(f32[128,256]{1,0:T(8,128)} %convolution_subtract_fusion.10) | copy-start | bytes 393220
  666.6 109.3 %copy-start.21 = (f32[256]{0:T(256)S(1)}, f32[256]{0:T(256)}, u32[]{:S(2)}) copy-start(f32[256]{0:T(256)} %get-tuple-element.248) | copy-start | bytes 3076
  666.6 109.4 %copy-start.22 = (u32[32]{0:T(128)S(1)}, u32[32]{0:T(128)}, u32[]{:S(2)}) copy-start(u32[32]{0:T(128)} %constant.320) | copy-start | bytes 388
  666.6 140.6 %copy-start.5 = (f32[1024,256]{1,0:T(8,128)S(1)}, f32[1024,256]{1,0:T(8,128)}, u32[]{:S(2)}) copy-start(f32[1024,256]{1,0:T(8,128)} %all-reduce.11.cloned.1.call-done) | copy-start | bytes 3145732
  667.7 139.6 %all-gather.10.cloned.1.call-start = ((), (), s32[]{:S(2)}) async-start(), calls=%async_computation.6 | async-start | bytes 1179648 | tf_op jit(solution)/shard_map/all_gather | solution.py:164
  775.8 164.1 %all-reduce.15.cloned.1.call-start = ((), (), s32[]{:S(2)}) async-start(), calls=%async_computation.7 | async-start | bytes 2097152 | tf_op jit(solution)/shard_map/psum | solution.py:16
  813.7 24.3 %slice-start = ((f32[1024,256]{1,0:T(8,128)}), f32[768,256]{1,0:T(8,128)S(1)}, s32[]{:S(2)}) async-start(f32[1024,256]{1,0:T(8,128)} %all-reduce.11.cloned.1.call-done), calls=%async_computation.10 | async-start | bytes 1572864 | tf_op jit(solution)/shard_map/slice | solution.py:184
  813.7 126.1 %copy-start.8 = (f32[128,256]{1,0:T(8,128)S(1)}, f32[128,256]{1,0:T(8,128)}, u32[]{:S(2)}) copy-start(f32[128,256]{1,0:T(8,128)} %convolution_subtract_fusion.9) | copy-start | bytes 393220
  813.8 128.3 %copy-start.6 = (f32[1024,256]{1,0:T(8,128)S(1)}, f32[1024,256]{1,0:T(8,128)}, u32[]{:S(2)}) copy-start(f32[1024,256]{1,0:T(8,128)} %all-reduce.13.cloned.1.call-done) | copy-start | bytes 3145732
  813.8 154.1 %all-gather.12.cloned.1.call-start = ((), (), s32[]{:S(2)}) async-start(), calls=%async_computation.8 | async-start | bytes 1179648 | tf_op jit(solution)/shard_map/all_gather | solution.py:164
  942.0 118.3 %all-reduce.17.cloned.1.call-start = ((), (), s32[]{:S(2)}) async-start(), calls=%async_computation.9 | async-start | bytes 2097152 | tf_op jit(solution)/shard_map/psum | solution.py:16
  (209 other events, 398.0 us)
Sparse Core Ops, SparseCore 0:
  471.3 18.7 reduce-scatter.1
  492.3 25.1 all-gather.5
  526.7 105.3 all-reduce.10
  634.3 23.8 all-gather.7
  667.8 105.8 all-reduce.12
  775.9 23.8 all-gather.9
  813.9 125.9 all-reduce.14
  942.1 24.1 all-gather.11
  1007.7 52.5 all-reduce.16
where the time goes:
time: 1110 us; the launch traced here: 1090 us
  waiting for transfers between devices  409 us (37%)
  local copies, waits for them, and re-layouts  350 us (32%)
  other arithmetic  196 us (18%)
  matrix products  64.9 us (6%)
  loops' own time  30.2 us (3%)
  blocking collectives  29.8 us (3%)
  between operations  14.4 us (1%)
    psum x4, waiting for transfers between devices, from_root(): return lax.psum(kept, axis)  340 us
    another operation x13, other arithmetic, on_device(): lax.linalg.triangular_solve(factored[first_row:end_row], gradient[first_r...  80.8 us
    mul x96, local copies, waits for them, and re-layouts, block_terms(): schur = schur + selector[view][:, None, None, :] * products[view][None]  77.7 us
    mul x80, local copies, waits for them, and re-layouts, block_terms(): schur = selector[0][:, None, None, :] * products[0][None]  61.6 us
    all_gather x4, waiting for transfers between devices, on_device(): column = lax.all_gather(held, ('region', 'row'), axis=0, tiled=True)  49.6 us
    dynamic_slice x32, local copies, waits for them, and re-layouts, block_step(): cam = lax.dynamic_slice_in_dim(cam_jac, start, BLOCK, 3)  35.4 us
    another operation x6, other arithmetic, panel_factor(): chol_block = jnp.linalg.cholesky(column[first_row:end_row])  34 us
    convert_element_type x16, local copies, waits for them, and re-layouts, block_terms(): jnp.einsum('krpb,kab->aprb', cam, pick, preferred_element_type=jnp.float32)  30.1 us
  transfers between devices with their start and end apart: 9, of which 7 were waited for; matrix products, arithmetic and copies ran while one was open for 7% of the time, Pallas kernels for 0%

commit v1 on v0

v1 whole, which is shorter than its diff:
```python
import functools

import jax
import jax.numpy as jnp
from jax import lax
from jax.experimental import pallas as pl
from jax.experimental.pallas import tpu as pltpu
from jax.sharding import PartitionSpec as P

SLAB_IMAGES = 4
BLOCK = 512
TILE = 128
EXTRA = 8
VMEM_LIMIT = 60 * 1024 * 1024

damping = 0.1
point_damping = 0.5

NT = (((1,), (1,)), ((), ()))


def point_terms(pts):
    views = len(pts)
    pairs = [(k, r) for k in range(views) for r in range(2)]

    def entry(left, right):
        return sum(pts[k][r][left] * pts[k][r][right] for k, r in pairs)

    d1 = jnp.sqrt(entry(0, 0) + point_damping)
    b1 = entry(1, 0) / d1
    bf = entry(2, 0) / d1
    d2 = jnp.sqrt(entry(1, 1) + point_damping - b1 * b1)
    b2 = (entry(2, 1) - bf * b1) / d2
    d3 = jnp.sqrt(entry(2, 2) + point_damping - bf * bf - b2 * b2)

    def solve(first, second, third):
        o1 = first / d1
        o2 = (second - b1 * o1) / d2
        o3 = (third - bf * o1 - b2 * o2) / d3
        return [o.astype(jnp.bfloat16).astype(jnp.float32) for o in (o1, o2, o3)]

    coef = {(k, r): solve(*pts[k][r][0:3]) for k, r in pairs}
    step = solve(*[entry(c, 3) for c in range(3)])
    return coef, step


def accumulate_kernel(regions, pos_ref, cam_ref, pts_ref, img_ref, out_ref, acc, rows, cols, dr, dc):
    views = cam_ref.shape[0]
    params = cam_ref.shape[2]
    block = cam_ref.shape[3]
    half = params // 2
    tile_rows = SLAB_IMAGES * half
    step = pl.program_id(0)
    count = pos_ref[0]
    row_at = pos_ref[1]
    col_at = pos_ref[2]

    @pl.when(step == 0)
    def _():
        acc[...] = jnp.zeros_like(acc)
        rows[tile_rows:, :] = jnp.zeros_like(rows[tile_rows:, :])
        dr[half:, :] = jnp.zeros_like(dr[half:, :])

    @pl.when(step * block < count)
    def _():
        slot = step * block + lax.broadcasted_iota(jnp.int32, (1, block), 1)
        live = slot < count
        pts = []
        for k in range(views):
            pts.append([])
            for r in range(2):
                wide = pts_ref[k, r].astype(jnp.float32)
                pts[k].append([wide[c : c + 1, :] for c in range(4)])
        coef, y = point_terms(pts)
        images = [img_ref[k : k + 1, :] for k in range(views)]

        def picks(image):
            return [(images[k] == image) & live for k in range(views)]

        def pick(masks, values):
            out = jnp.zeros_like(values[0])
            for mask, value in zip(masks, values):
                out = jnp.where(mask, value, out)
            return out

        def chosen(image):
            masks = picks(image)
            c = [
                [pick(masks, [coef[k, r][m] for k in range(views)]) for r in range(2)]
                for m in range(3)
            ]
            return masks, c

        zero = jnp.zeros((15, block), jnp.float32)
        for m in range(3):
            rows[tile_rows : tile_rows + 16, m * block : (m + 1) * block] = jnp.concatenate(
                [y[m], zero], axis=0
            ).astype(jnp.bfloat16)

        sub = 16
        col_masks, col_c = chosen(col_at)
        for r in range(2):
            err = pick(col_masks, [pts[k][r][3] for k in range(views)])
            dr[half : half + 16, r * block : (r + 1) * block] = jnp.concatenate(
                [err, zero], axis=0
            ).astype(jnp.bfloat16)

        def widen(mask):
            return jnp.broadcast_to(mask.astype(jnp.int32), (sub, block)) != 0

        def products(jac, c):
            return [jac[0] * c[m][0] + jac[1] * c[m][1] for m in range(3)]

        def col_chunk(i, _):
            at = pl.multiple_of(i * sub, sub)
            jac = []
            for r in range(2):
                j = [cam_ref[k, r, pl.ds(at, sub), :].astype(jnp.float32) for k in range(views)]
                picked = pick([widen(m) for m in col_masks], j)
                dc[pl.ds(at, sub), r * block : (r + 1) * block] = picked.astype(jnp.bfloat16)
                jac.append(picked)
            for m, value in enumerate(products(jac, col_c)):
                cols[pl.ds(at, sub), m * block : (m + 1) * block] = value.astype(jnp.bfloat16)
            return 0

        lax.fori_loop(0, params // sub, col_chunk, 0)

        row_chosen = [chosen(a) for a in range(SLAB_IMAGES)]

        def row_chunk(i, _):
            at = pl.multiple_of(i * sub, sub)
            src = pl.multiple_of(row_at * half + i * sub, sub)
            j = [
                [cam_ref[k, r, pl.ds(src, sub), :].astype(jnp.float32) for k in range(views)]
                for r in range(2)
            ]
            for a in range(SLAB_IMAGES):
                masks, c = row_chosen[a]
                wide = [widen(m) for m in masks]
                jac = [
                    jnp.where(wide[0], j[r][0], jnp.where(wide[1], j[r][1], j[r][2]))
                    for r in range(2)
                ]
                for m, value in enumerate(products(jac, c)):
                    rows[pl.ds(a * half + at, sub), m * block : (m + 1) * block] = value.astype(
                        jnp.bfloat16
                    )
            return 0

        lax.fori_loop(0, half // sub, row_chunk, 0)
        dr[0:half, :] = dc[pl.ds(pl.multiple_of(row_at * half, half), half), :]
        acc[...] -= lax.dot_general(
            rows[...], cols[...], NT, preferred_element_type=jnp.float32
        )
        direct = lax.dot_general(dr[...], dc[...], NT, preferred_element_type=jnp.float32)
        at = pl.ds(pl.multiple_of(col_at * half, half), half)
        acc[at, :] += direct[0:half]
        acc[tile_rows : tile_rows + 16, :] += direct[half : half + 16]

    @pl.when(step == pl.num_programs(0) - 1)
    def _():
        chunk = tile_rows // regions
        for r in range(regions):
            out_ref[r, 0:chunk, :] = acc[r * chunk : (r + 1) * chunk, :]
            out_ref[r, chunk : chunk + EXTRA, :] = acc[tile_rows : tile_rows + EXTRA, :]


def accumulate(cam_jac, point_rows, track_images, pos, regions):
    views, _, params, slots = cam_jac.shape
    block = min(BLOCK, slots)
    half = params // 2
    tile_rows = SLAB_IMAGES * half
    chunk = tile_rows // regions

    def at(i, pos_ref):
        return jnp.minimum(i, (pos_ref[0] - 1) // block)

    return pl.pallas_call(
        functools.partial(accumulate_kernel, regions),
        out_shape=jax.ShapeDtypeStruct((regions, chunk + EXTRA, params), jnp.float32),
        grid_spec=pltpu.PrefetchScalarGridSpec(
            num_scalar_prefetch=1,
            grid=(slots // block,),
            in_specs=[
                pl.BlockSpec((views, 2, params, block), lambda i, p: (0, 0, 0, at(i, p))),
                pl.BlockSpec((views, 2, 4, block), lambda i, p: (0, 0, 0, at(i, p))),
                pl.BlockSpec((views, block), lambda i, p: (0, at(i, p))),
            ],
            out_specs=pl.BlockSpec((regions, chunk + EXTRA, params), lambda i, p: (0, 0, 0)),
            scratch_shapes=[
                pltpu.VMEM((tile_rows + 16, params), jnp.float32),
                pltpu.VMEM((tile_rows + 16, 3 * block), jnp.bfloat16),
                pltpu.VMEM((params, 3 * block), jnp.bfloat16),
                pltpu.VMEM((half + 16, 2 * block), jnp.bfloat16),
                pltpu.VMEM((params, 2 * block), jnp.bfloat16),
            ],
        ),
        compiler_params=pltpu.CompilerParams(
            dimension_semantics=("arbitrary",), vmem_limit_bytes=VMEM_LIMIT
        ),
        name="accumulate",
    )(pos, cam_jac, point_rows, track_images)


def eliminate(tile):
    groups = TILE // 8
    sub = lax.broadcasted_iota(jnp.int32, (8, TILE), 0)
    lane = lax.broadcasted_iota(jnp.int32, (8, TILE), 1)
    d = [tile[8 * g : 8 * g + 8, :] for g in range(groups)]
    e = [(lane == sub + 8 * g).astype(jnp.float32) for g in range(groups)]
    for j in range(TILE):
        g, s = j // 8, j % 8
        row = d[g][s : s + 1, :]
        row_e = e[g][s : s + 1, :]
        pivot = jnp.broadcast_to(row[:, j : j + 1], (1, TILE))
        inv = 1.0 / pivot
        srow = jnp.broadcast_to(row * inv, (8, TILE))
        srow_e = jnp.broadcast_to(row_e * inv, (8, TILE))
        root = lax.rsqrt(pivot)
        for i in range(g, groups):
            col = jnp.broadcast_to(d[i][:, j : j + 1], (8, TILE))
            if i == g:
                col = jnp.where(sub > s, col, 0.0)
            new_d = d[i] - col * srow
            new_e = e[i] - col * srow_e
            if i == g:
                new_d = jnp.where(sub == s, d[i] * root, new_d)
                new_e = jnp.where(sub == s, e[i] * root, new_e)
            d[i] = new_d
            e[i] = new_e
    u = jnp.concatenate([jnp.where(lane >= sub + 8 * g, d[g], 0.0) for g in range(groups)], axis=0)
    return u, jnp.concatenate(e, axis=0)


def factor_kernel(regions, params, pos_ref, all_ref, factor_ref, solved_ref, a_ref, linv_ref):
    total = SLAB_IMAGES * params
    half = params // 2
    chunk = SLAB_IMAGES * half // regions
    for r in range(regions):
        for c in range(2):
            first = (r * chunk) // half * params + c * half + (r * chunk) % half
            for j in range(SLAB_IMAGES):
                a_ref[first : first + chunk, j * params : (j + 1) * params] = all_ref[
                    (r * 2 + c) * SLAB_IMAGES + j, 0:chunk, :
                ]
    for j in range(SLAB_IMAGES):
        a_ref[total : total + EXTRA, j * params : (j + 1) * params] = all_ref[
            j, chunk : chunk + EXTRA, :
        ]
    panels = total // TILE
    eye_r = lax.broadcasted_iota(jnp.int32, (TILE, TILE), 0)
    eye_c = lax.broadcasted_iota(jnp.int32, (TILE, TILE), 1)
    damp = jnp.where(eye_r == eye_c, damping, 0.0).astype(jnp.float32)

    def panel(n, _):
        at = pl.ds(pl.multiple_of(n * TILE, TILE), TILE)
        upper, linv = eliminate(a_ref[at, at] + damp)
        a_ref[at, at] = upper.T
        linv_ref[...] = linv
        for s in range(panels):

            @pl.when(n == s)
            def _():
                lo = s * TILE
                hi = lo + TILE
                below = lax.dot_general(
                    a_ref[hi : total + EXTRA, lo:hi],
                    linv_ref[...],
                    NT,
                    precision=lax.Precision.HIGHEST,
                    preferred_element_type=jnp.float32,
                )
                a_ref[hi : total + EXTRA, lo:hi] = below
                col = hi
                while col < total:
                    width = 2 * TILE if col % (2 * TILE) == 0 else TILE
                    a_ref[col : total + EXTRA, col : col + width] -= lax.dot_general(
                        a_ref[col : total + EXTRA, lo:hi],
                        a_ref[col : col + width, lo:hi],
                        NT,
                        precision=lax.Precision.HIGHEST,
                        preferred_element_type=jnp.float32,
                    )
                    col += width

        return 0

    lax.fori_loop(0, panels, panel, 0)
    row_block = factor_ref.shape[0]
    first_row = pl.multiple_of(pos_ref[3] * row_block, row_block)
    first_col = pl.multiple_of(pos_ref[2] * params, params)
    held = a_ref[pl.ds(first_row, row_block), pl.ds(first_col, params)]
    at_row = first_row + lax.broadcasted_iota(jnp.int32, held.shape, 0)
    at_col = first_col + lax.broadcasted_iota(jnp.int32, held.shape, 1)
    factor_ref[...] = jnp.where(at_row >= at_col, held, 0.0)
    solved_ref[...] = a_ref[total : total + EXTRA, :]


def factorize(everything, pos, regions, params, row_block):
    total = SLAB_IMAGES * params
    return pl.pallas_call(
        functools.partial(factor_kernel, regions, params),
        out_shape=(
            jax.ShapeDtypeStruct((row_block, params), jnp.float32),
            jax.ShapeDtypeStruct((EXTRA, total), jnp.float32),
        ),
        in_specs=[
            pl.BlockSpec(memory_space=pltpu.SMEM),
            pl.BlockSpec(memory_space=pltpu.VMEM),
        ],
        out_specs=(
            pl.BlockSpec(memory_space=pltpu.VMEM),
            pl.BlockSpec(memory_space=pltpu.VMEM),
        ),
        scratch_shapes=[
            pltpu.VMEM((total + EXTRA, total), jnp.float32),
            pltpu.VMEM((TILE, TILE), jnp.float32),
        ],
        compiler_params=pltpu.CompilerParams(vmem_limit_bytes=VMEM_LIMIT),
        name="factorize",
    )(pos, everything)


def on_device(cam_jac, point_rows, track_images, track_counts):
    regions = lax.axis_size("region")
    row_count = lax.axis_size("row")
    region_at = lax.axis_index("region")
    row_at = lax.axis_index("row")
    col_at = lax.axis_index("col")
    params = cam_jac.shape[2]
    row_block = SLAB_IMAGES * params // (regions * row_count)
    pos = jnp.stack(
        [track_counts[region_at], row_at, col_at, region_at * row_count + row_at]
    ).astype(jnp.int32)
    tile = accumulate(cam_jac, point_rows, track_images, pos, regions)
    summed = lax.psum_scatter(tile, "region", scatter_dimension=0, tiled=False)
    everything = lax.all_gather(summed, ("region", "row", "col"), axis=0, tiled=False)
    factor, solved = factorize(everything, pos, regions, params, row_block)
    return (factor, solved[0])


def solution(mesh):
    in_specs = (
        P(None, None, None, "region"),
        P(None, None, None, "region"),
        P(None, "region"),
        P(),
    )
    out_specs = (P(("region", "row"), "col"), P())
    return jax.shard_map(
        on_device, mesh=mesh, in_specs=in_specs, out_specs=out_specs, check_vma=False
    )
```

time: 1110 us -> 234 us (0.21); the launches traced: 1090 us -> 232 us
  local copies, waits for them, and re-layouts: 350 us -> 2.59 us
  waiting for transfers between devices: 409 us -> 101 us
  other arithmetic: 196 us -> 1.21 us
  Pallas kernels: 0 us -> 113 us
  matrix products: 64.9 us -> 0 us
  loops' own time: 30.2 us -> 0 us
  blocking collectives: 29.8 us -> 0 us
    psum x4 -> x0, waiting for transfers between devices: 340 us -> none  [from_root(): return lax.psum(kept, axis)]
    mul x176 -> x0, local copies, waits for them, and re-layouts: 139 us -> none  [the longest x96 77.7 us: block_terms(): schur = schur + selector[view][:, None, None, :] * products[view][None]]
    another operation x51 -> x1, other arithmetic: 125 us -> 1.21 us  [on_device(): jnp.stack([track_counts[region_at], row_at, col_at, region_at * row_count...]
    pallas_call x0 -> x2, Pallas kernels: none -> 113 us  [the longest x1 105 us: factorize(): pl.pallas_call(functools.partial(factor_kernel, regions, params), out_sha...]
    dynamic_slice x160 -> x0, local copies, waits for them, and re-layouts: 101 us -> none  [the longest x32 35.4 us: block_step(): cam = lax.dynamic_slice_in_dim(cam_jac, start, BLOCK, 3)]
    dot_general x86 -> x0, matrix products: 62.2 us -> none  [the longest x16 17.5 us: block_step(): lax.dot_general(diag_rows, diag_col, contract, preferred_element_type=jnp...]
    convert_element_type x80 -> x0, local copies, waits for them, and re-layouts: 38.6 us -> none  [the longest x16 30.1 us: block_terms(): jnp.einsum('krpb,kab->aprb', cam, pick, preferred_element_type=jnp.float32)]
    convert_element_type x114 -> x0, other arithmetic: 37.9 us -> none  [the longest x32 28.8 us: block_terms(): schur = schur.astype(jnp.bfloat16)]
  transfers between devices with their start and end apart: 9 -> 2, of which waited for: 7 -> 2; matrix products, arithmetic and copies ran while one was open for 7% -> 0% of each run, Pallas kernels for 0% -> 0%
where the time goes in v1:
time: 234 us; the launch traced here: 232 us
  Pallas kernels  113 us (48%)
  waiting for transfers between devices  101 us (43%)
  between operations  14 us (6%)
  local copies, waits for them, and re-layouts  2.59 us (1%)
    pallas_call x1, Pallas kernels, factorize(): pl.pallas_call(functools.partial(factor_kernel, regions, params), out_sha...  105 us
    all_gather x1, waiting for transfers between devices, on_device(): lax.all_gather(summed, ('region', 'row', 'col'), axis=0, tiled=False)  67 us
    reduce_scatter x1, waiting for transfers between devices, on_device(): summed = lax.psum_scatter(tile, 'region', scatter_dimension=0, tiled=False)  34 us
    pallas_call x1, Pallas kernels, accumulate(): pl.pallas_call(functools.partial(accumulate_kernel, regions), out_shape=j...  8.28 us
  transfers between devices with their start and end apart: 2, of which 2 were waited for; matrix products, arithmetic and copies ran while one was open for 0% of the time, Pallas kernels for 0%

profile of v1, /device:TPU:15, one launch (start us, length us, event | category | flops | bytes accessed | tf_op | source)
XLA Modules:
  0.0 232.0 jit_solution(5291630402712620805)
XLA Ops:
  7.2 0.0 reduce-scatter.2.cloned.1.call-start
  7.2 1.2 dynamic_slice.3
  8.5 1.2 pad_add_fusion.pos_ref
  9.7 8.3 %accumulate.1 = f32[4,136,256]{2,1,0:T(8,128)} custom-call(s32[4]{0:T(128)} %pad_add_fusion.pos_ref, bf16[3,2,256,4096]{3,2,1,0:T(8,128)(2,1)} %cam_ref.1, bf16[3,2,4,4096]{3,2,1,0:T(4,128)(2,1)} %pts_ref.1, s32[3,4096]{1,0:T(4,128)} %img_ref.1), custom_call_target="tpu_custom_call" | custom-call | tf_op jit(solution)/shard_map/accumulate/pallas_call | solution.py:178
  18.0 0.0 reduce-scatter.2.cloned.1.call-update
  18.0 0.0 all-gather.2.cloned.1.call-start
  18.0 34.0 %reduce-scatter.2.cloned.1.call-done = f32[1,136,256]{2,1,0:T(8,128)} async-done(((f32[4,136,256]{2,1,0:T(8,128)}), f32[1,136,256]{2,1,0:T(8,128)}) %reduce-scatter.2.cloned.1.call-update) | async-done | bytes 139280 | tf_op jit(solution)/shard_map/reduce_scatter | solution.py:336
  52.0 0.0 all-gather.2.cloned.1.call-update
  52.1 67.0 %all-gather.2.cloned.1.call-done.all_ref = f32[32,136,256]{2,1,0:T(8,128)} async-done(((f32[1,136,256]{2,1,0:T(8,128)}), f32[32,136,256]{2,1,0:T(8,128)}) %all-gather.2.cloned.1.call-update) | async-done | bytes 4456464 | tf_op jit(solution)/shard_map/all_gather | solution.py:337
  119.0 104.8 %factorize.1 = (f32[128,256]{1,0:T(8,128)}, f32[8,1024]{1,0:T(8,128)}) custom-call(s32[4]{0:T(128)} %pad_add_fusion.pos_ref, f32[32,136,256]{2,1,0:T(8,128)} %all-gather.2.cloned.1.call-done.all_ref), custom_call_target="tpu_custom_call" | custom-call | tf_op jit(solution)/shard_map/factorize/pallas_call | solution.py:301
  223.8 1.4 slice.3
Async XLA Ops:
  7.2 44.9 %reduce-scatter.2.cloned.1.call-start = ((), (), s32[]{:S(2)}) async-start(), calls=%async_computation.1 | async-start | bytes 696320 | tf_op jit(solution)/shard_map/reduce_scatter | solution.py:336
  18.0 101.1 %all-gather.2.cloned.1.call-start = ((), (), s32[]{:S(2)}) async-start(), calls=%async_computation.2 | async-start | bytes 4595712 | tf_op jit(solution)/shard_map/all_gather | solution.py:337
Sparse Core Ops, SparseCore 0:
  18.1 33.8 reduce-scatter.1
  54.9 64.0 all-gather.1

commit v2 on v1

--- a/solution.py
+++ b/solution.py
@@ -11,6 +11,7 @@
 BLOCK = 512
 TILE = 128
 EXTRA = 8
+PIVOTS = 8
 VMEM_LIMIT = 60 * 1024 * 1024
 
 damping = 0.1
@@ -208,26 +209,52 @@
     lane = lax.broadcasted_iota(jnp.int32, (8, TILE), 1)
     d = [tile[8 * g : 8 * g + 8, :] for g in range(groups)]
     e = [(lane == sub + 8 * g).astype(jnp.float32) for g in range(groups)]
-    for j in range(TILE):
+    for j in range(0, TILE, PIVOTS):
         g, s = j // 8, j % 8
-        row = d[g][s : s + 1, :]
-        row_e = e[g][s : s + 1, :]
-        pivot = jnp.broadcast_to(row[:, j : j + 1], (1, TILE))
-        inv = 1.0 / pivot
-        srow = jnp.broadcast_to(row * inv, (8, TILE))
-        srow_e = jnp.broadcast_to(row_e * inv, (8, TILE))
-        root = lax.rsqrt(pivot)
+        ids = range(PIVOTS)
+        rd = [d[g][s + q : s + q + 1, :] for q in ids]
+        re = [e[g][s + q : s + q + 1, :] for q in ids]
+        block = {
+            (p, q): jnp.broadcast_to(rd[p][:, j + q : j + q + 1], (1, TILE))
+            for p in ids
+            for q in ids
+            if q >= p
+        }
+        low, inv = {}, []
+        for p in ids:
+            inv.append(1.0 / block[p, p])
+            for q in range(p + 1, PIVOTS):
+                low[q, p] = block[p, q] * inv[p]
+            for q in range(p + 1, PIVOTS):
+                for r in range(q, PIVOTS):
+                    block[q, r] = block[q, r] - low[q, p] * block[p, r]
+                rd[q] = rd[q] - low[q, p] * rd[p]
+                re[q] = re[q] - low[q, p] * re[p]
+        roots = [lax.rsqrt(block[p, p]) for p in ids]
+        wd = [rd[p] * inv[p] for p in ids]
+        we = [re[p] * inv[p] for p in ids]
+        for q in reversed(ids):
+            for p in range(q):
+                wd[p] = wd[p] - low[q, p] * wd[q]
+                we[p] = we[p] - low[q, p] * we[q]
+        wd = [jnp.broadcast_to(w, (8, TILE)) for w in wd]
+        we = [jnp.broadcast_to(w, (8, TILE)) for w in we]
         for i in range(g, groups):
-            col = jnp.broadcast_to(d[i][:, j : j + 1], (8, TILE))
+            if i == g and s + PIVOTS == 8:
+                new_d, new_e = d[i], e[i]
+            else:
+                new_d, new_e = d[i], e[i]
+                for p in ids:
+                    col = jnp.broadcast_to(d[i][:, j + p : j + p + 1], (8, TILE))
+                    if i == g:
+                        col = jnp.where(sub >= s + PIVOTS, col, 0.0)
+                    new_d = new_d - col * wd[p]
+                    new_e = new_e - col * we[p]
             if i == g:
-                col = jnp.where(sub > s, col, 0.0)
-            new_d = d[i] - col * srow
-            new_e = e[i] - col * srow_e
-            if i == g:
-                new_d = jnp.where(sub == s, d[i] * root, new_d)
-                new_e = jnp.where(sub == s, e[i] * root, new_e)
-            d[i] = new_d
-            e[i] = new_e
+                for p in ids:
+                    new_d = jnp.where(sub == s + p, rd[p] * roots[p], new_d)
+                    new_e = jnp.where(sub == s + p, re[p] * roots[p], new_e)
+            d[i], e[i] = new_d, new_e
     u = jnp.concatenate([jnp.where(lane >= sub + 8 * g, d[g], 0.0) for g in range(groups)], axis=0)
     return u, jnp.concatenate(e, axis=0)
 
@@ -239,13 +266,13 @@
     for r in range(regions):
         for c in range(2):
             first = (r * chunk) // half * params + c * half + (r * chunk) % half
-            for j in range(SLAB_IMAGES):
+            for j in range((r * chunk) // half + 1):
                 a_ref[first : first + chunk, j * params : (j + 1) * params] = all_ref[
                     (r * 2 + c) * SLAB_IMAGES + j, 0:chunk, :
                 ]
     for j in range(SLAB_IMAGES):
         a_ref[total : total + EXTRA, j * params : (j + 1) * params] = all_ref[
-            j, chunk : chunk + EXTRA, :
+            j * half // chunk * 2 * SLAB_IMAGES + j, chunk : chunk + EXTRA, :
         ]
     panels = total // TILE
     eye_r = lax.broadcasted_iota(jnp.int32, (TILE, TILE), 0)
@@ -321,6 +348,154 @@
     )(pos, everything)
 
 
+def exchange_kernel(regions, tile_ref, all_ref, recv, mine, sum_send, sum_recv, sends, arrived):
+    half = recv.shape[2] // 2
+    chunk = SLAB_IMAGES * half // regions
+    region_at = lax.axis_index("region")
+    row_at = lax.axis_index("row")
+    col_at = lax.axis_index("col")
+
+    def device(region, row, col):
+        return {"region": region, "row": row, "col": col}
+
+    def plus(at, by, size):
+        return lax.rem(at + by, size)
+
+    def needed(region, col):
+        return (region * chunk) // half >= col
+
+    def index(region, row, col):
+        return (region * 2 + row) * SLAB_IMAGES + col
+
+    partner = device(region_at, 1 - row_at, col_at)
+    along = [device(plus(region_at, d, regions), row_at, col_at) for d in range(1, regions)]
+    across = [device(region_at, row_at, plus(col_at, d, SLAB_IMAGES)) for d in range(1, SLAB_IMAGES)]
+    barrier = pltpu.get_barrier_semaphore()
+    for peer in [partner] + along + across:
+        pl.semaphore_signal(barrier, inc=1, device_id=peer, device_id_type=pl.DeviceIdType.MESH)
+    pl.semaphore_wait(barrier, regions + SLAB_IMAGES - 1)
+
+    def part(d):
+        to = plus(region_at, d, regions)
+        return to, pltpu.make_async_remote_copy(
+            src_ref=tile_ref.at[to],
+            dst_ref=recv.at[d - 1],
+            send_sem=sum_send.at[d - 1],
+            recv_sem=sum_recv.at[d - 1],
+            device_id=device(to, row_at, col_at),
+            device_id_type=pl.DeviceIdType.MESH,
+        )
+
+    for d in range(1, regions):
+        to, copy = part(d)
+
+        @pl.when(needed(to, col_at))
+        def _():
+            copy.start()
+
+    me = index(region_at, row_at, col_at)
+
+    @pl.when(needed(region_at, col_at))
+    def _():
+        for d in range(1, regions):
+            part(d)[1].wait_recv()
+        total = tile_ref[region_at]
+        for d in range(1, regions):
+            total = total + recv[d - 1]
+        mine[...] = total
+        all_ref[me] = total
+
+    for d in range(1, regions):
+        to, copy = part(d)
+
+        @pl.when(needed(to, col_at))
+        def _():
+            copy.wait_send()
+
+    started = []
+
+    def send(when, src, block, peer):
+        copy = pltpu.make_async_remote_copy(
+            src_ref=src,
+            dst_ref=all_ref.at[block],
+            send_sem=sends.at[len(started)],
+            recv_sem=arrived.at[block],
+            device_id=peer,
+            device_id_type=pl.DeviceIdType.MESH,
+        )
+        started.append((when, copy))
+
+        @pl.when(when)
+        def _():
+            copy.start()
+
+    def arrive(when, block):
+        copy = pltpu.make_async_remote_copy(
+            src_ref=all_ref.at[block],
+            dst_ref=all_ref.at[block],
+            send_sem=sends.at[0],
+            recv_sem=arrived.at[block],
+            device_id=partner,
+            device_id_type=pl.DeviceIdType.MESH,
+        )
+
+        @pl.when(when)
+        def _():
+            copy.wait_recv()
+
+    ok = needed(region_at, col_at)
+    for peer in along + across + [partner]:
+        send(ok, mine, me, peer)
+    for d in range(1, regions):
+        origin = plus(region_at, d, regions)
+        block = index(origin, row_at, col_at)
+        ok = needed(origin, col_at)
+        arrive(ok, block)
+        for peer in across + [partner]:
+            send(ok, all_ref.at[block], block, peer)
+    for rd in range(regions):
+        for cd in range(1, SLAB_IMAGES):
+            origin = plus(region_at, rd, regions)
+            col = plus(col_at, cd, SLAB_IMAGES)
+            block = index(origin, row_at, col)
+            ok = needed(origin, col)
+            arrive(ok, block)
+            send(ok, all_ref.at[block], block, partner)
+    for rd in range(regions):
+        for cd in range(SLAB_IMAGES):
+            origin = plus(region_at, rd, regions)
+            col = plus(col_at, cd, SLAB_IMAGES)
+            arrive(needed(origin, col), index(origin, 1 - row_at, col))
+    for when, copy in started:
+
+        @pl.when(when)
+        def _():
+            copy.wait_send()
+
+
+def exchange(tile):
+    regions, depth, params = tile.shape
+    blocks = regions * 2 * SLAB_IMAGES
+    return pl.pallas_call(
+        functools.partial(exchange_kernel, regions),
+        out_shape=jax.ShapeDtypeStruct((blocks, depth, params), jnp.float32),
+        in_specs=[pl.BlockSpec(memory_space=pltpu.VMEM)],
+        out_specs=pl.BlockSpec(memory_space=pltpu.VMEM),
+        scratch_shapes=[
+            pltpu.VMEM((regions - 1, depth, params), jnp.float32),
+            pltpu.VMEM((depth, params), jnp.float32),
+            pltpu.SemaphoreType.DMA((regions - 1,)),
+            pltpu.SemaphoreType.DMA((regions - 1,)),
+            pltpu.SemaphoreType.DMA((blocks,)),
+            pltpu.SemaphoreType.DMA((blocks,)),
+        ],
+        compiler_params=pltpu.CompilerParams(
+            collective_id=0, has_side_effects=True, vmem_limit_bytes=VMEM_LIMIT
+        ),
+        name="exchange",
+    )(tile)
+
+
 def on_device(cam_jac, point_rows, track_images, track_counts):
     regions = lax.axis_size("region")
     row_count = lax.axis_size("row")
@@ -333,8 +508,7 @@
         [track_counts[region_at], row_at, col_at, region_at * row_count + row_at]
     ).astype(jnp.int32)
     tile = accumulate(cam_jac, point_rows, track_images, pos, regions)
-    summed = lax.psum_scatter(tile, "region", scatter_dimension=0, tiled=False)
-    everything = lax.all_gather(summed, ("region", "row", "col"), axis=0, tiled=False)
+    everything = exchange(tile)
     factor, solved = factorize(everything, pos, regions, params, row_block)
     return (factor, solved[0])
 

time: 234 us -> 126 us (0.54)
  waiting for transfers between devices: 101 us -> 0 us
  between operations: 14 us -> 0.65 us
  Pallas kernels: 113 us -> 121 us
    all_gather x1 -> x0, waiting for transfers between devices: 67 us -> none  [on_device(): lax.all_gather(summed, ('region', 'row', 'col'), axis=0, tiled=False)]
    pallas_call x1, Pallas kernels: 105 us -> 49.3 us  [factorize(): pl.pallas_call(functools.partial(factor_kernel, regions, params), out_sha...]
    pallas_call x0 -> x1, Pallas kernels: none -> 49 us  [exchange(): pl.pallas_call(functools.partial(exchange_kernel, regions), out_shape=jax...]
    reduce_scatter x1 -> x0, waiting for transfers between devices: 34 us -> none  [on_device(): summed = lax.psum_scatter(tile, 'region', scatter_dimension=0, tiled=False)]
    pallas_call x1, Pallas kernels: 8.28 us -> 23 us  [accumulate(): pl.pallas_call(functools.partial(accumulate_kernel, regions), out_shape=j...]
  transfers between devices with their start and end apart: 2 -> 0, of which waited for: 2 -> 0; matrix products, arithmetic and copies ran while one was open for 0% -> 0% of each run, Pallas kernels for 0% -> 0%
where the time goes in v2:
time: 126 us
  Pallas kernels  121 us (96%)
  local copies, waits for them, and re-layouts  2.62 us (2%)
    pallas_call x1, Pallas kernels, factorize(): pl.pallas_call(functools.partial(factor_kernel, regions, params), out_sha...  49.3 us
    pallas_call x1, Pallas kernels, exchange(): pl.pallas_call(functools.partial(exchange_kernel, regions), out_shape=jax...  49 us
    pallas_call x1, Pallas kernels, accumulate(): pl.pallas_call(functools.partial(accumulate_kernel, regions), out_shape=j...  23 us

profile of v2, /device:TPU:15, one launch (start us, length us, event | category | flops | bytes accessed | tf_op | source)
XLA Modules:
  0.0 125.7 jit_solution(6248253436577382434)
XLA Ops:
  0.6 1.3 %dynamic_slice.3 = s32[1]{0:T(128)} dynamic-slice(s32[4]{0:T(128)} %param.7, s32[]{:T(128)S(6)} %select_n.3), dynamic_slice_sizes={1} | dynamic-slice | bytes 12 | tf_op jit(solution)/shard_map/dynamic_slice | solution.py:508
  1.9 1.2 pad_add_fusion.pos_ref
  3.1 23.0 %accumulate.1.tile_ref = f32[4,136,256]{2,1,0:T(8,128)} custom-call(s32[4]{0:T(128)} %pad_add_fusion.pos_ref, bf16[3,2,256,4096]{3,2,1,0:T(8,128)(2,1)} %cam_ref.1, bf16[3,2,4,4096]{3,2,1,0:T(4,128)(2,1)} %pts_ref.1, s32[3,4096]{1,0:T(4,128)} %img_ref.1), custom_call_target="tpu_custom_call" | custom-call | tf_op jit(solution)/shard_map/accumulate/pallas_call | solution.py:179
  26.1 49.0 %exchange.1.all_ref = f32[32,136,256]{2,1,0:T(8,128)} custom-call(f32[4,136,256]{2,1,0:T(8,128)} %accumulate.1.tile_ref), custom_call_target="tpu_custom_call" | custom-call | tf_op jit(solution)/shard_map/exchange/pallas_call | solution.py:479
  75.1 49.3 %factorize.1 = (f32[128,256]{1,0:T(8,128)}, f32[8,1024]{1,0:T(8,128)}) custom-call(s32[4]{0:T(128)} %pad_add_fusion.pos_ref, f32[32,136,256]{2,1,0:T(8,128)} %exchange.1.all_ref), custom_call_target="tpu_custom_call" | custom-call | tf_op jit(solution)/shard_map/factorize/pallas_call | solution.py:328
  124.4 1.4 %slice.3 = f32[1,1024]{1,0:T(1,128)} slice(f32[8,1024]{1,0:T(8,128)} %get-tuple-element.5), slice={[0:1], [0:1024]} | slice | bytes 8192 | tf_op jit(solution)/shard_map/slice | solution.py:513

commit v3 on v2

--- a/solution.py
+++ b/solution.py
@@ -52,9 +52,9 @@
     half = params // 2
     tile_rows = SLAB_IMAGES * half
     step = pl.program_id(0)
-    count = pos_ref[0]
-    row_at = pos_ref[1]
-    col_at = pos_ref[2]
+    count = pos_ref[lax.axis_index("region")]
+    row_at = lax.axis_index("row")
+    col_at = lax.axis_index("col")
 
     @pl.when(step == 0)
     def _():
@@ -174,7 +174,7 @@
     chunk = tile_rows // regions
 
     def at(i, pos_ref):
-        return jnp.minimum(i, (pos_ref[0] - 1) // block)
+        return jnp.minimum(i, (pos_ref[lax.axis_index("region")] - 1) // block)
 
     return pl.pallas_call(
         functools.partial(accumulate_kernel, regions),
@@ -259,7 +259,7 @@
     return u, jnp.concatenate(e, axis=0)
 
 
-def factor_kernel(regions, params, pos_ref, all_ref, factor_ref, solved_ref, a_ref, linv_ref):
+def factor_kernel(regions, params, all_ref, factor_ref, solved_ref, a_ref, linv_ref):
     total = SLAB_IMAGES * params
     half = params // 2
     chunk = SLAB_IMAGES * half // regions
@@ -314,27 +314,26 @@
 
     lax.fori_loop(0, panels, panel, 0)
     row_block = factor_ref.shape[0]
-    first_row = pl.multiple_of(pos_ref[3] * row_block, row_block)
-    first_col = pl.multiple_of(pos_ref[2] * params, params)
+    first_row = pl.multiple_of(
+        (lax.axis_index("region") * 2 + lax.axis_index("row")) * row_block, row_block
+    )
+    first_col = pl.multiple_of(lax.axis_index("col") * params, params)
     held = a_ref[pl.ds(first_row, row_block), pl.ds(first_col, params)]
     at_row = first_row + lax.broadcasted_iota(jnp.int32, held.shape, 0)
     at_col = first_col + lax.broadcasted_iota(jnp.int32, held.shape, 1)
     factor_ref[...] = jnp.where(at_row >= at_col, held, 0.0)
-    solved_ref[...] = a_ref[total : total + EXTRA, :]
-
-
-def factorize(everything, pos, regions, params, row_block):
+    solved_ref[...] = a_ref[total, :]
+
+
+def factorize(everything, regions, params, row_block):
     total = SLAB_IMAGES * params
     return pl.pallas_call(
         functools.partial(factor_kernel, regions, params),
         out_shape=(
             jax.ShapeDtypeStruct((row_block, params), jnp.float32),
-            jax.ShapeDtypeStruct((EXTRA, total), jnp.float32),
+            jax.ShapeDtypeStruct((total,), jnp.float32),
         ),
-        in_specs=[
-            pl.BlockSpec(memory_space=pltpu.SMEM),
-            pl.BlockSpec(memory_space=pltpu.VMEM),
-        ],
+        in_specs=[pl.BlockSpec(memory_space=pltpu.VMEM)],
         out_specs=(
             pl.BlockSpec(memory_space=pltpu.VMEM),
             pl.BlockSpec(memory_space=pltpu.VMEM),
@@ -345,7 +344,7 @@
         ],
         compiler_params=pltpu.CompilerParams(vmem_limit_bytes=VMEM_LIMIT),
         name="factorize",
-    )(pos, everything)
+    )(everything)
 
 
 def exchange_kernel(regions, tile_ref, all_ref, recv, mine, sum_send, sum_recv, sends, arrived):
@@ -369,9 +368,13 @@
 
     partner = device(region_at, 1 - row_at, col_at)
     along = [device(plus(region_at, d, regions), row_at, col_at) for d in range(1, regions)]
-    across = [device(region_at, row_at, plus(col_at, d, SLAB_IMAGES)) for d in range(1, SLAB_IMAGES)]
+    side = col_at + 1 - 2 * lax.rem(col_at, 2)
+    over = plus(col_at, 2, SLAB_IMAGES)
+    corner = SLAB_IMAGES - 1 - col_at
+    across = [device(region_at, row_at, side), device(region_at, row_at, over)]
+    far = device(region_at, row_at, corner)
     barrier = pltpu.get_barrier_semaphore()
-    for peer in [partner] + along + across:
+    for peer in [partner, far] + along + across:
         pl.semaphore_signal(barrier, inc=1, device_id=peer, device_id_type=pl.DeviceIdType.MESH)
     pl.semaphore_wait(barrier, regions + SLAB_IMAGES - 1)
 
@@ -404,13 +407,6 @@
             total = total + recv[d - 1]
         mine[...] = total
         all_ref[me] = total
-
-    for d in range(1, regions):
-        to, copy = part(d)
-
-        @pl.when(needed(to, col_at))
-        def _():
-            copy.wait_send()
 
     started = []
 
@@ -454,18 +450,32 @@
         for peer in across + [partner]:
             send(ok, all_ref.at[block], block, peer)
     for rd in range(regions):
-        for cd in range(1, SLAB_IMAGES):
-            origin = plus(region_at, rd, regions)
-            col = plus(col_at, cd, SLAB_IMAGES)
+        origin = plus(region_at, rd, regions)
+        for turn, col in enumerate((side, over)):
             block = index(origin, row_at, col)
             ok = needed(origin, col)
             arrive(ok, block)
+            onward = jnp.logical_and(ok, lax.rem(origin, 2) == turn)
+            send(onward, all_ref.at[block], block, across[1 - turn])
             send(ok, all_ref.at[block], block, partner)
+    for rd in range(regions):
+        origin = plus(region_at, rd, regions)
+        block = index(origin, row_at, corner)
+        ok = needed(origin, corner)
+        arrive(ok, block)
+        send(ok, all_ref.at[block], block, partner)
     for rd in range(regions):
         for cd in range(SLAB_IMAGES):
             origin = plus(region_at, rd, regions)
             col = plus(col_at, cd, SLAB_IMAGES)
             arrive(needed(origin, col), index(origin, 1 - row_at, col))
+    for d in range(1, regions):
+        to, copy = part(d)
+
+        @pl.when(needed(to, col_at))
+        def _():
+            copy.wait_send()
+
     for when, copy in started:
 
         @pl.when(when)
@@ -486,7 +496,7 @@
             pltpu.VMEM((depth, params), jnp.float32),
             pltpu.SemaphoreType.DMA((regions - 1,)),
             pltpu.SemaphoreType.DMA((regions - 1,)),
-            pltpu.SemaphoreType.DMA((blocks,)),
+            pltpu.SemaphoreType.DMA((blocks + regions,)),
             pltpu.SemaphoreType.DMA((blocks,)),
         ],
         compiler_params=pltpu.CompilerParams(
@@ -499,18 +509,12 @@
 def on_device(cam_jac, point_rows, track_images, track_counts):
     regions = lax.axis_size("region")
     row_count = lax.axis_size("row")
-    region_at = lax.axis_index("region")
-    row_at = lax.axis_index("row")
-    col_at = lax.axis_index("col")
     params = cam_jac.shape[2]
     row_block = SLAB_IMAGES * params // (regions * row_count)
-    pos = jnp.stack(
-        [track_counts[region_at], row_at, col_at, region_at * row_count + row_at]
-    ).astype(jnp.int32)
-    tile = accumulate(cam_jac, point_rows, track_images, pos, regions)
+    tile = accumulate(cam_jac, point_rows, track_images, track_counts, regions)
     everything = exchange(tile)
-    factor, solved = factorize(everything, pos, regions, params, row_block)
-    return (factor, solved[0])
+    factor, solved = factorize(everything, regions, params, row_block)
+    return (factor, solved)
 
 
 def solution(mesh):

time: 126 us -> 120 us (0.952)
  local copies, waits for them, and re-layouts: 2.62 us -> 0 us
  Pallas kernels: 121 us -> 119 us
    pallas_call x1, Pallas kernels: 23 us -> 11.6 us  [accumulate(): pl.pallas_call(functools.partial(accumulate_kernel, regions), out_shape=j...]
    pallas_call x1, Pallas kernels: 49 us -> 57.6 us  [exchange(): pl.pallas_call(functools.partial(exchange_kernel, regions), out_shape=jax...]
    slice x1 -> x0, local copies, waits for them, and re-layouts: 1.35 us -> none  [on_device(): return (factor, solved[0])]
    dynamic_slice x1 -> x0, local copies, waits for them, and re-layouts: 1.27 us -> none  [on_device(): track_counts[region_at]]
where the time goes in v3:
time: 120 us; the launch traced here: 119 us
  Pallas kernels  119 us (99%)
    pallas_call x1, Pallas kernels, exchange(): pl.pallas_call(functools.partial(exchange_kernel, regions), out_shape=jax...  57.6 us
    pallas_call x1, Pallas kernels, factorize(): pl.pallas_call(functools.partial(factor_kernel, regions, params), out_sha...  49.3 us
    pallas_call x1, Pallas kernels, accumulate(): pl.pallas_call(functools.partial(accumulate_kernel, regions), out_shape=j...  11.6 us

profile of v3, /device:TPU:15, one launch (start us, length us, event | category | flops | bytes accessed | tf_op | source)
XLA Modules:
  0.0 119.2 jit_solution(6870395967402842475)
XLA Ops:
  0.6 11.6 %accumulate.1.tile_ref = f32[4,136,256]{2,1,0:T(8,128)} custom-call(s32[4]{0:T(128)} %pos_ref.1, bf16[3,2,256,4096]{3,2,1,0:T(8,128)(2,1)} %cam_ref.1, bf16[3,2,4,4096]{3,2,1,0:T(4,128)(2,1)} %pts_ref.1, s32[3,4096]{1,0:T(4,128)} %img_ref.1), custom_call_target="tpu_custom_call" | custom-call | tf_op jit(solution)/shard_map/accumulate/pallas_call | solution.py:179
  12.3 57.6 %exchange.1.all_ref = f32[32,136,256]{2,1,0:T(8,128)} custom-call(f32[4,136,256]{2,1,0:T(8,128)} %accumulate.1.tile_ref), custom_call_target="tpu_custom_call" | custom-call | tf_op jit(solution)/shard_map/exchange/pallas_call | solution.py:489
  69.9 49.3 %factorize.1 = (f32[128,256]{1,0:T(8,128)}, f32[1024]{0:T(1024)}) custom-call(f32[32,136,256]{2,1,0:T(8,128)} %exchange.1.all_ref), custom_call_target="tpu_custom_call" | custom-call | tf_op jit(solution)/shard_map/factorize/pallas_call | solution.py:330
